TPU v7x, 512 devices: a whole 4x4x16 slice. The times are simulated.
512 devices in a mesh: dp: 8 (over x, core), expert: 64 (over y, z).
Axes of the slice: x: 4, y: 4, z: 16, core: 2. Of those that a mesh axis runs over, the one named last changes fastest.
Arguments:
- tokens: bfloat16 [8192, 2048], P('expert', 'dp'), may hold values from -6 to 6
- cotangent: bfloat16 [8192, 2048], P('expert', 'dp'), may hold values from -6 to 6
- routes: int32 [8192, 8], P('expert'), may hold values from 0 to 63, as said below
- mix_weights: float32 [8192, 8], P('expert'), may hold values from 0.05 to 0.5
- w_gate: bfloat16 [64, 2048, 384], P('expert', 'dp'), may hold values from -0.125 to 0.125
- w_up: bfloat16 [64, 2048, 384], P('expert', 'dp'), may hold values from -0.125 to 0.125
- w_down: bfloat16 [64, 384, 2048], P('expert', None, 'dp'), may hold values from -0.3125 to 0.3125
Outputs:
- mixed: bfloat16 [8192, 2048], P('expert', 'dp')
- token_grad: bfloat16 [8192, 2048], P('expert', 'dp')
- gate_grad: float32 [64, 2048, 384], P('expert', 'dp')
- up_grad: float32 [64, 2048, 384], P('expert', 'dp')
- down_grad: float32 [64, 384, 2048], P('expert', None, 'dp')
Inputs may be any that keep to these rules, and one draw needn't show every extreme that they name: `routes`: each row names 8 different experts. In each aligned block of 128 rows at most 32 rows name the same expert, and some block reaches that. In all, at most 1792 rows name one expert, and some expert is named by exactly that many.
All inputs are finite; a program needn't handle non-finite values.
Results may differ from a plain program's by a relative error of at most 0.023.
Values may be sent and summed in bfloat16 or wider, within the bound.
A program may use at most 64 MiB of HBM per device.

v0:
```python
import jax
import jax.numpy as jnp
from jax import lax
from jax.sharding import PartitionSpec as P


def contract(left_side, right_side, left_dim, right_dim):
    return lax.dot_general(
        left_side,
        right_side,
        (((left_dim,), (right_dim,)), ((), ())),
        preferred_element_type=jnp.float32,
    )


def silu_parts(gate_in):
    logistic = jax.nn.sigmoid(gate_in)
    return (gate_in * logistic, logistic * (1.0 + gate_in * (1.0 - logistic)))


def shards(tokens, cotangent, routes, mix_weights, w_gate, w_up, w_down):
    tok_rows, width_dev = tokens.shape
    picks_per = routes.shape[1]
    owner_count = lax.axis_size("expert")
    send_cap = 2 * tok_rows * picks_per // owner_count
    expert_cap = 7 * tok_rows * picks_per // 4
    slot_total = owner_count * send_cap
    gate_matrix = w_gate[0]
    up_matrix = w_up[0]
    down_matrix = w_down[0]
    flat_routes = routes.reshape(-1)
    owner_ids = jnp.arange(owner_count, dtype=jnp.int32)
    onehot = (owner_ids[:, None] == flat_routes[None, :]).astype(jnp.int32)
    earlier = jnp.cumsum(onehot, axis=1) - onehot
    rank_in = jnp.sum(earlier * onehot, axis=0)
    slot_index = flat_routes * send_cap + rank_in
    sent_counts = jnp.sum(onehot, axis=1).reshape(owner_count, 1)

    def to_slots(values):
        empty_rows = jnp.zeros((slot_total, width_dev), values.dtype)
        return empty_rows.at[slot_index].set(values).reshape(owner_count, send_cap, width_dev)

    x_slots = to_slots(jnp.repeat(tokens, picks_per, axis=0))
    scaled = mix_weights[:, :, None] * cotangent[:, None, :].astype(jnp.float32)
    grad_slots = to_slots(scaled.astype(jnp.bfloat16).reshape(tok_rows * picks_per, width_dev))
    got_tokens, got_counts = (
        lax.all_to_all(x_slots, "expert", split_axis=0, concat_axis=0, tiled=True),
        lax.all_to_all(sent_counts, "expert", split_axis=0, concat_axis=0, tiled=True),
    )
    counts = got_counts[:, 0]
    starts = jnp.cumsum(counts) - counts
    position = jnp.arange(send_cap, dtype=jnp.int32)
    target = jnp.where(
        position[None, :] < counts[:, None], starts[:, None] + position[None, :], expert_cap
    ).reshape(-1)
    fetch_row = jnp.minimum(target, expert_cap - 1)

    def pack_rows(slot_rows):
        empty_rows = jnp.zeros((expert_cap, width_dev), slot_rows.dtype)
        return empty_rows.at[target].set(slot_rows.reshape(slot_total, width_dev), mode="drop")

    def unpack(rows_in):
        return rows_in[fetch_row].reshape(owner_count, send_cap, width_dev)

    packed_x = pack_rows(got_tokens)
    gate_part = jnp.dot(packed_x, gate_matrix, preferred_element_type=jnp.float32)
    up_part = jnp.dot(packed_x, up_matrix, preferred_element_type=jnp.float32)
    gate_in, up_in = (
        lax.psum(gate_part.astype(jnp.bfloat16), "dp").astype(jnp.float32),
        lax.psum(up_part.astype(jnp.bfloat16), "dp").astype(jnp.float32),
    )
    activated, slope_silu = silu_parts(gate_in)
    hidden_act = (activated * up_in).astype(jnp.bfloat16)
    expert_out = jnp.dot(hidden_act, down_matrix, preferred_element_type=jnp.float32).astype(
        jnp.bfloat16
    )
    back_out = lax.all_to_all(unpack(expert_out), "expert", split_axis=0, concat_axis=0, tiled=True)
    got_grad = lax.all_to_all(grad_slots, "expert", split_axis=0, concat_axis=0, tiled=True)
    packed_grad = pack_rows(got_grad)
    back_hidden = lax.psum(
        contract(packed_grad, down_matrix, 1, 1).astype(jnp.bfloat16), "dp"
    ).astype(jnp.float32)
    gate_back = (back_hidden * up_in * slope_silu).astype(jnp.bfloat16)
    up_back = (back_hidden * activated).astype(jnp.bfloat16)
    row_grad = (contract(gate_back, gate_matrix, 1, 1) + contract(up_back, up_matrix, 1, 1)).astype(
        jnp.bfloat16
    )
    gate_grad = contract(packed_x, gate_back, 0, 0)
    up_grad = contract(packed_x, up_back, 0, 0)
    down_grad = contract(hidden_act, packed_grad, 0, 0)
    back_grad = lax.all_to_all(unpack(row_grad), "expert", split_axis=0, concat_axis=0, tiled=True)

    def collect(returned):
        picked = returned.reshape(slot_total, width_dev)[slot_index]
        return picked.reshape(tok_rows, picks_per, width_dev).astype(jnp.float32)

    mixed = jnp.sum(mix_weights[:, :, None] * collect(back_out), axis=1).astype(jnp.bfloat16)
    token_grad = jnp.sum(collect(back_grad), axis=1).astype(jnp.bfloat16)
    return (mixed, token_grad, gate_grad[None], up_grad[None], down_grad[None])


def solution(mesh):
    placed = (
        P("expert", "dp"),
        P("expert", "dp"),
        P("expert", None),
        P("expert", None),
        P("expert", "dp", None),
        P("expert", "dp", None),
        P("expert", None, "dp"),
    )
    return jax.shard_map(
        shards,
        mesh=mesh,
        in_specs=placed,
        out_specs=(
            P("expert", "dp"),
            P("expert", "dp"),
            P("expert", "dp", None),
            P("expert", "dp", None),
            P("expert", None, "dp"),
        ),
        check_vma=False,
    )
```

profile of v0, /device:TPU:6, one launch (start us, length us, event | category | flops | bytes accessed | tf_op | source)
XLA Modules:
  0.0 434.1 jit_solution(10336787646805802478)
XLA Ops:
  7.2 0.8 copy.41
  8.1 0.1 convert_reduce_fusion
  8.3 0.7 copy.42
  9.0 18.7 %all-to-all-start = ((s32[64,1,1]{2,1,0:T(1,128)}), s32[64,1,1]{2,1,0:T(1,128)S(1)}, u32[]{:S(2)}, u32[]{:S(2)}) async-start(s32[64,1,1]{2,1,0:T(1,128)} %copy.42), calls=%async_computation | async-start | bytes 65536 | tf_op jit(solution)/shard_map/all_to_all | solution.py:48
  27.7 0.7 broadcast_multiply_fusion
  28.5 0.1 copy.44
  28.6 0.1 mul.69
  28.7 18.0 %reduce-window.19 = s32[64,8,128]{2,1,0:T(8,128)S(1)} reduce-window(s32[64,8,128]{2,1,0:T(8,128)S(1)} %fusion.25, s32[]{:T(128)} %constant.9.clone.1), window={size=1x1x128 pad=0_0x0_0x127_0}, to_apply=%region_2.3 | reduce-window | flops 8323072 | bytes 524292 | tf_op jit(solution)/shard_map/reduce-window.1
  46.7 0.1 slice.16
  46.9 0.1 copy.46
  47.1 0.1 select_reduce_fusion
  47.3 0.1 copy.40
  47.6 6.5 %scatter_custom_fusion.2 = bf16[2048,256]{1,0:T(8,128)(2,1)} fusion(s32[1024]{0:T(1024)S(1)} %bitcast.75, f32[128,256]{1,0:T(8,128)S(1)} %convert_element_type.70, f32[1024]{0:T(1024)S(1)} %mul.74, bf16[]{:T(256)} %constant.8.clone.1), kind=kCustom, calls=%fused_computation.36 | custom fusion | flops 524288 | bytes 1183746 | tf_op jit(solution)/shard_map/scatter | solution.py:41
  54.1 15.1 %all-to-all-start.3 = ((bf16[64,32,256]{2,1,0:T(8,128)(2,1)}), bf16[64,32,256]{2,1,0:T(8,128)(2,1)S(1)}, u32[]{:S(2)}, u32[]{:S(2)}) async-start(bf16[64,32,256]{2,1,0:T(8,128)(2,1)} %bitcast.17), calls=%async_computation.3 | async-start | bytes 2097152 | tf_op jit(solution)/shard_map/all_to_all | solution.py:78
  69.3 6.0 %scatter_custom_fusion = bf16[2048,256]{1,0:T(8,128)(2,1)} fusion(s32[1024]{0:T(1024)S(1)} %bitcast.76, bf16[]{:T(256)} %constant.8.clone.1, bf16[128,256]{1,0:T(8,128)(2,1)S(1)} %copy-done.15), kind=kCustom, calls=%fused_computation.38 | custom fusion | bytes 1114114 | tf_op jit(solution)/shard_map/scatter | solution.py:41
  75.3 47.2 %all-to-all-done.3 = bf16[64,32,256]{2,1,0:T(8,128)(2,1)S(1)} async-done(((bf16[64,32,256]{2,1,0:T(8,128)(2,1)}), bf16[64,32,256]{2,1,0:T(8,128)(2,1)S(1)}, u32[]{:S(2)}, u32[]{:S(2)}) %all-to-all-start.3) | async-done | bytes 1048608 | tf_op jit(solution)/shard_map/all_to_all | solution.py:78
  122.5 6.8 %all-to-all-start.1 = ((bf16[64,32,256]{2,1,0:T(8,128)(2,1)}), bf16[64,32,256]{2,1,0:T(8,128)(2,1)S(1)}, u32[]{:S(2)}, u32[]{:S(2)}) async-start(bf16[64,32,256]{2,1,0:T(8,128)(2,1)} %bitcast.7), calls=%async_computation.1 | async-start | bytes 2097152 | tf_op jit(solution)/shard_map/all_to_all | solution.py:47
  129.3 0.2 all-reduce.3.cloned.1.call-start
  129.6 0.1 reduce-window.18
  129.7 0.1 reduce.3
  129.8 1.2 reduce.2
  131.2 9.5 %scatter_custom_fusion.3 = bf16[1792,256]{1,0:T(8,128)(2,1)S(1)} fusion(s32[2048]{0:T(1024)S(1)} %bitcast.78, bf16[2048,256]{1,0:T(8,128)(2,1)S(1)} %bitcast.69, bf16[]{:T(256)} %constant.8.clone.1), kind=kCustom, calls=%fused_computation.44 | custom fusion | bytes 917506 | tf_op jit(solution)/shard_map/scatter | solution.py:60
  140.8 42.3 %all-to-all-done.1 = bf16[64,32,256]{2,1,0:T(8,128)(2,1)S(1)} async-done(((bf16[64,32,256]{2,1,0:T(8,128)(2,1)}), bf16[64,32,256]{2,1,0:T(8,128)(2,1)S(1)}, u32[]{:S(2)}, u32[]{:S(2)}) %all-to-all-start.1) | async-done | bytes 1048608 | tf_op jit(solution)/shard_map/all_to_all | solution.py:47
  183.1 9.5 %scatter_custom_fusion.1 = bf16[1792,256]{1,0:T(8,128)(2,1)S(1)} fusion(s32[2048]{0:T(1024)S(1)} %bitcast.79, bf16[2048,256]{1,0:T(8,128)(2,1)S(1)} %bitcast.70, bf16[]{:T(256)} %constant.8.clone.1), kind=kCustom, calls=%fused_computation.46 | custom fusion | bytes 917506 | tf_op jit(solution)/shard_map/scatter | solution.py:60
  192.6 1.7 convolution_convert_fusion.1
  194.3 1.8 convolution_convert_fusion.2
  196.1 1.7 convolution_convert_fusion
  197.9 77.5 %all-reduce.3.cloned.1.call-done = (bf16[1792,384]{1,0:T(8,128)(2,1)}, bf16[1792,384]{1,0:T(8,128)(2,1)}, bf16[1792,384]{1,0:T(8,128)(2,1)}) async-done(((bf16[1792,384]{1,0:T(8,128)(2,1)}, bf16[1792,384]{1,0:T(8,128)(2,1)}, bf16[1792,384]{1,0:T(8,128)(2,1)}), (bf16[1792,384]{1,0:T(8,128)(2,1)}, bf16[1792,384]{1,0:T(8,128)(2,1)}, bf16[1792,384]{1,0:T(8,128)(2,1)})) %all-reduce.3.cloned.1.call-update) | async-done | bytes 4128784 | tf_op jit(solution)/shard_map/psum | solution.py:70
  275.4 3.9 fusion.3
  279.3 0.7 fusion.30
  280.0 0.4 copy-done.3
  280.3 0.4 copy-done.5
  280.8 0.7 fusion.9
  281.5 9.0 %gather_fusion.2 = bf16[2048,256]{1,0:T(8,128)(2,1)} fusion(bf16[1792,256]{1,0:T(8,128)(2,1)S(1)} %fusion.9, s32[2048]{0:T(1024)S(1)} %broadcast_clamp_fusion), kind=kCustom, calls=%fused_computation.2 | custom fusion | bytes 2105344 | tf_op jit(solution)/shard_map/gather | solution.py:63
  290.4 15.6 %all-to-all-start.4 = ((bf16[64,32,256]{2,1,0:T(8,128)(2,1)}), bf16[64,32,256]{2,1,0:T(8,128)(2,1)S(1)}, u32[]{:S(2)}, u32[]{:S(2)}) async-start(bf16[64,32,256]{2,1,0:T(8,128)(2,1)} %bitcast.68), calls=%async_computation.4 | async-start | bytes 2097152 | tf_op jit(solution)/shard_map/all_to_all | solution.py:91
  306.1 1.6 convolution_convert_fusion.3
  307.7 9.0 %gather_fusion = bf16[2048,256]{1,0:T(8,128)(2,1)} fusion(bf16[1792,256]{1,0:T(8,128)(2,1)S(1)} %convolution_convert_fusion.3, s32[2048]{0:T(1024)S(1)} %broadcast_clamp_fusion), kind=kCustom, calls=%fused_computation | custom fusion | bytes 2105344 | tf_op jit(solution)/shard_map/gather | solution.py:63
  316.6 40.8 %all-to-all-done.4 = bf16[64,32,256]{2,1,0:T(8,128)(2,1)S(1)} async-done(((bf16[64,32,256]{2,1,0:T(8,128)(2,1)}), bf16[64,32,256]{2,1,0:T(8,128)(2,1)S(1)}, u32[]{:S(2)}, u32[]{:S(2)}) %all-to-all-start.4) | async-done | bytes 1048608 | tf_op jit(solution)/shard_map/all_to_all | solution.py:91
  357.4 10.5 %all-to-all-start.2 = ((bf16[64,32,256]{2,1,0:T(8,128)(2,1)}), bf16[64,32,256]{2,1,0:T(8,128)(2,1)S(1)}, u32[]{:S(2)}, u32[]{:S(2)}) async-start(bf16[64,32,256]{2,1,0:T(8,128)(2,1)} %bitcast.67), calls=%async_computation.2 | async-start | bytes 2097152 | tf_op jit(solution)/shard_map/all_to_all | solution.py:77
  368.0 2.9 convolution_bitcast_fusion.1
  370.9 1.4 convolution_bitcast_fusion.2
  372.3 0.2 copy-done.9
  372.5 1.3 convolution_bitcast_fusion
  373.8 3.9 gather_fusion.3
  377.7 1.0 bitcast_reduce_fusion
  378.7 43.6 %all-to-all-done.2 = bf16[64,32,256]{2,1,0:T(8,128)(2,1)S(1)} async-done(((bf16[64,32,256]{2,1,0:T(8,128)(2,1)}), bf16[64,32,256]{2,1,0:T(8,128)(2,1)S(1)}, u32[]{:S(2)}, u32[]{:S(2)}) %all-to-all-start.2) | async-done | bytes 1048608 | tf_op jit(solution)/shard_map/all_to_all | solution.py:77
  422.3 3.9 gather_fusion.1
  426.2 1.0 fusion.10
  (48 shorter events, 0.7 us)
Async XLA Ops:
  7.2 187.1 %copy-start = (bf16[1,256,384]{2,1,0:T(8,128)(2,1)S(1)}, bf16[1,256,384]{2,1,0:T(8,128)(2,1)}, u32[]{:S(2)}) copy-start(bf16[1,256,384]{2,1,0:T(8,128)(2,1)} %param.11) | copy-start | bytes 589828
  7.2 40.1 %copy-start.16 = (f32[128,8]{0,1:T(8,128)S(1)}, f32[128,8]{0,1:T(8,128)}, u32[]{:S(2)}) copy-start(f32[128,8]{0,1:T(8,128)} %param.10) | copy-start | bytes 12292
  7.2 40.3 %copy-start.14 = (bf16[128,256]{1,0:T(8,128)(2,1)S(1)}, bf16[128,256]{1,0:T(8,128)(2,1)}, u32[]{:S(2)}) copy-start(bf16[128,256]{1,0:T(8,128)(2,1)} %param.8) | copy-start | bytes 196612
  9.0 45.1 %all-to-all-start = ((s32[64,1,1]{2,1,0:T(1,128)}), s32[64,1,1]{2,1,0:T(1,128)S(1)}, u32[]{:S(2)}, u32[]{:S(2)}) async-start(s32[64,1,1]{2,1,0:T(1,128)} %copy.42), calls=%async_computation | async-start | bytes 65536 | tf_op jit(solution)/shard_map/all_to_all | solution.py:48
  47.4 6.7 %copy-start.12 = (f32[128,8]{1,0:T(8,128)}, f32[128,8]{1,0:T(8,128)S(1)}, u32[]{:S(2)}) copy-start(f32[128,8]{1,0:T(8,128)S(1)} %copy.40) | copy-start | bytes 12292
  47.5 21.7 %copy-start.15 = (bf16[128,256]{1,0:T(8,128)(2,1)S(1)}, bf16[128,256]{1,0:T(8,128)(2,1)}, u32[]{:S(2)}) copy-start(bf16[128,256]{1,0:T(8,128)(2,1)} %param.7) | copy-start | bytes 196612
  54.1 68.4 %all-to-all-start.3 = ((bf16[64,32,256]{2,1,0:T(8,128)(2,1)}), bf16[64,32,256]{2,1,0:T(8,128)(2,1)S(1)}, u32[]{:S(2)}, u32[]{:S(2)}) async-start(bf16[64,32,256]{2,1,0:T(8,128)(2,1)} %bitcast.17), calls=%async_computation.3 | async-start | bytes 2097152 | tf_op jit(solution)/shard_map/all_to_all | solution.py:78
  122.5 60.5 %all-to-all-start.1 = ((bf16[64,32,256]{2,1,0:T(8,128)(2,1)}), bf16[64,32,256]{2,1,0:T(8,128)(2,1)S(1)}, u32[]{:S(2)}, u32[]{:S(2)}) async-start(bf16[64,32,256]{2,1,0:T(8,128)(2,1)} %bitcast.7), calls=%async_computation.1 | async-start | bytes 2097152 | tf_op jit(solution)/shard_map/all_to_all | solution.py:47
  129.3 63.2 %copy-start.10 = (bf16[1,256,384]{2,1,0:T(8,128)(2,1)S(1)}, bf16[1,256,384]{2,1,0:T(8,128)(2,1)}, u32[]{:S(2)}) copy-start(bf16[1,256,384]{2,1,0:T(8,128)(2,1)} %param.12) | copy-start | bytes 589828
  129.3 146.1 %all-reduce.3.cloned.1.call-start = ((), (), s32[]{:S(2)}) async-start(), calls=%async_computation.5 | async-start | bytes 8257536 | tf_op jit(solution)/shard_map/psum | solution.py:70
  140.7 55.3 %copy-start.8 = (bf16[1792,256]{1,0:T(8,128)(2,1)}, bf16[1792,256]{1,0:T(8,128)(2,1)S(1)}, u32[]{:S(2)}) copy-start(bf16[1792,256]{1,0:T(8,128)(2,1)S(1)} %scatter_custom_fusion.3) | copy-start | bytes 2752516
  192.6 3.5 copy-start.1
  194.3 1.8 copy-start.11
  279.3 1.1 copy-start.3
  279.3 1.5 copy-start.5
  279.3 26.8 %copy-start.6 = (bf16[1792,384]{1,0:T(8,128)(2,1)}, bf16[1792,384]{1,0:T(8,128)(2,1)S(1)}, u32[]{:S(2)}) copy-start(bf16[1792,384]{1,0:T(8,128)(2,1)S(1)} %get-tuple-element.10) | copy-start | bytes 4128772
  290.4 67.0 %all-to-all-start.4 = ((bf16[64,32,256]{2,1,0:T(8,128)(2,1)}), bf16[64,32,256]{2,1,0:T(8,128)(2,1)S(1)}, u32[]{:S(2)}, u32[]{:S(2)}) async-start(bf16[64,32,256]{2,1,0:T(8,128)(2,1)} %bitcast.68), calls=%async_computation.4 | async-start | bytes 2097152 | tf_op jit(solution)/shard_map/all_to_all | solution.py:91
  316.6 51.4 %copy-start.2 = (bf16[1792,256]{1,0:T(8,128)(2,1)S(1)}, bf16[1792,256]{1,0:T(8,128)(2,1)}, u32[]{:S(2)}) copy-start(bf16[1792,256]{1,0:T(8,128)(2,1)} %copy-done.1) | copy-start | bytes 2752516
  357.4 64.8 %all-to-all-start.2 = ((bf16[64,32,256]{2,1,0:T(8,128)(2,1)}), bf16[64,32,256]{2,1,0:T(8,128)(2,1)S(1)}, u32[]{:S(2)}, u32[]{:S(2)}) async-start(bf16[64,32,256]{2,1,0:T(8,128)(2,1)} %bitcast.67), calls=%async_computation.2 | async-start | bytes 2097152 | tf_op jit(solution)/shard_map/all_to_all | solution.py:77
  368.0 2.9 copy-start.4
  370.9 1.4 copy-start.7
  370.9 1.6 copy-start.9
  422.3 3.9 copy-start.13
Sparse Core Ops, SparseCore 0:
  198.0 77.3 all-reduce.2
where the time goes:
time: 435 us; the launch traced here: 434 us
  waiting for transfers between devices  251 us (58%)
  starting transfers between devices  67.1 us (15%)
  local copies, waits for them, and re-layouts  54.5 us (13%)
  other arithmetic  33 us (8%)
  between operations  14.4 us (3%)
  matrix products  13.7 us (3%)
    psum x1, waiting for transfers between devices, shards(): lax.psum(up_part.astype(jnp.bfloat16), 'dp').astype(jnp.float32)  77.5 us
    all_to_all x1, waiting for transfers between devices, shards(): lax.all_to_all(grad_slots, 'expert', split_axis=0, concat_axis=0, tiled=T...  47.2 us
    all_to_all x1, waiting for transfers between devices, shards(): lax.all_to_all(unpack(expert_out), 'expert', split_axis=0, concat_axis=0,...  43.6 us
    all_to_all x1, waiting for transfers between devices, shards(): lax.all_to_all(x_slots, 'expert', split_axis=0, concat_axis=0, tiled=True)  42.3 us
    all_to_all x1, waiting for transfers between devices, shards(): lax.all_to_all(unpack(row_grad), 'expert', split_axis=0, concat_axis=0, t...  40.8 us
    scatter x2, local copies, waits for them, and re-layouts, pack_rows(): empty_rows.at[target]  19 us
    all_to_all x1, starting transfers between devices, shards(): lax.all_to_all(sent_counts, 'expert', split_axis=0, concat_axis=0, tiled=...  18.7 us
    another operation x4, other arithmetic  18.2 us
  transfers between devices with their start and end apart: 6, of which 5 were waited for; matrix products, arithmetic and copies ran while one was open for 15% of the time, Pallas kernels for 0%

commit v1 on v0

--- a/solution.py
+++ b/solution.py
@@ -67,7 +67,7 @@
     up_part = jnp.dot(packed_x, up_matrix, preferred_element_type=jnp.float32)
     gate_in, up_in = (
         lax.psum(gate_part.astype(jnp.bfloat16), "dp").astype(jnp.float32),
-        lax.psum(up_part.astype(jnp.bfloat16), "dp").astype(jnp.float32),
+        jnp.sum(lax.all_gather(up_part.astype(jnp.bfloat16), "dp"), axis=0).astype(jnp.float32),
     )
     activated, slope_silu = silu_parts(gate_in)
     hidden_act = (activated * up_in).astype(jnp.bfloat16)

time: 435 us -> 446 us (1.025)
  blocking collectives: 0 us -> 60.3 us
  waiting for transfers between devices: 251 us -> 203 us
  starting transfers between devices: 67.1 us -> 60.2 us
  other arithmetic: 33 us -> 38.3 us
    all_to_all x0 -> x1, blocking collectives: none -> 60.3 us  [shards(): lax.all_to_all(grad_slots, 'expert', split_axis=0, concat_axis=0, tiled=T...]
    all_to_all x1 -> x0, waiting for transfers between devices: 47.2 us -> none  [shards(): lax.all_to_all(grad_slots, 'expert', split_axis=0, concat_axis=0, tiled=T...]
    all_to_all x1 -> x0, starting transfers between devices: 15.1 us -> none  [shards(): lax.all_to_all(grad_slots, 'expert', split_axis=0, concat_axis=0, tiled=T...]
    psum x1, waiting for transfers between devices: 77.5 us -> 66.8 us  [shards(): lax.psum(gate_part.astype(jnp.bfloat16), 'dp').astype(jnp.float32)]
    all_to_all x1, waiting for transfers between devices: 42.3 us -> 51.6 us  [shards(): lax.all_to_all(x_slots, 'expert', split_axis=0, concat_axis=0, tiled=True)]
    all_to_all x1, starting transfers between devices: 6.81 us -> 15.3 us  [shards(): lax.all_to_all(x_slots, 'expert', split_axis=0, concat_axis=0, tiled=True)]
    reduce_sum x0 -> x1, other arithmetic: none -> 6.54 us  [shards(): jnp.sum(lax.all_gather(up_part.astype(jnp.bfloat16), 'dp'), axis=0)]
  transfers between devices with their start and end apart: 6 -> 6, of which waited for: 5 -> 4; matrix products, arithmetic and copies ran while one was open for 15% -> 17% of each run, Pallas kernels for 0% -> 0%
where the time goes in v1:
time: 446 us; the launch traced here: 445 us
  waiting for transfers between devices  203 us (46%)
  blocking collectives  60.3 us (14%)
  starting transfers between devices  60.2 us (13%)
  local copies, waits for them, and re-layouts  55.3 us (12%)
  other arithmetic  38.3 us (9%)
  between operations  14.4 us (3%)
  matrix products  13.7 us (3%)
    psum x1, waiting for transfers between devices, shards(): lax.psum(gate_part.astype(jnp.bfloat16), 'dp').astype(jnp.float32)  66.8 us
    all_to_all x1, blocking collectives, shards(): lax.all_to_all(grad_slots, 'expert', split_axis=0, concat_axis=0, tiled=T...  60.3 us
    all_to_all x1, waiting for transfers between devices, shards(): lax.all_to_all(x_slots, 'expert', split_axis=0, concat_axis=0, tiled=True)  51.6 us
    all_to_all x1, waiting for transfers between devices, shards(): lax.all_to_all(unpack(expert_out), 'expert', split_axis=0, concat_axis=0,...  43.3 us
    all_to_all x1, waiting for transfers between devices, shards(): lax.all_to_all(unpack(row_grad), 'expert', split_axis=0, concat_axis=0, t...  41.3 us
    scatter x2, local copies, waits for them, and re-layouts, pack_rows(): empty_rows.at[target]  19.2 us
    all_to_all x1, starting transfers between devices, shards(): lax.all_to_all(sent_counts, 'expert', split_axis=0, concat_axis=0, tiled=...  18.7 us
    another operation x4, other arithmetic  18.2 us
  transfers between devices with their start and end apart: 6, of which 4 were waited for; matrix products, arithmetic and copies ran while one was open for 17% of the time, Pallas kernels for 0%

profile of v1, /device:TPU:6, one launch (start us, length us, event | category | flops | bytes accessed | tf_op | source)
XLA Modules:
  0.0 445.2 jit_solution(12896489023878251440)
XLA Ops:
  7.2 0.8 copy.41
  8.1 0.1 convert_reduce_fusion
  8.3 0.7 copy.42
  9.0 18.7 %all-to-all-start = ((s32[64,1,1]{2,1,0:T(1,128)}), s32[64,1,1]{2,1,0:T(1,128)S(1)}, u32[]{:S(2)}, u32[]{:S(2)}) async-start(s32[64,1,1]{2,1,0:T(1,128)} %copy.42), calls=%async_computation | async-start | bytes 65536 | tf_op jit(solution)/shard_map/all_to_all | solution.py:48
  27.7 0.7 broadcast_multiply_fusion
  28.5 0.1 copy.44
  28.6 0.1 mul.69
  28.7 18.0 %reduce-window.19 = s32[64,8,128]{2,1,0:T(8,128)S(1)} reduce-window(s32[64,8,128]{2,1,0:T(8,128)S(1)} %fusion.25, s32[]{:T(128)} %constant.9.clone.1), window={size=1x1x128 pad=0_0x0_0x127_0}, to_apply=%region_2.3 | reduce-window | flops 8323072 | bytes 524292 | tf_op jit(solution)/shard_map/reduce-window.1
  46.7 0.1 slice.16
  46.9 0.1 copy.46
  47.1 0.1 select_reduce_fusion
  47.3 6.0 %scatter_custom_fusion = bf16[2048,256]{1,0:T(8,128)(2,1)} fusion(s32[1024]{0:T(1024)S(1)} %bitcast.78, bf16[]{:T(256)} %constant.8.clone.1, bf16[128,256]{1,0:T(8,128)(2,1)S(1)} %copy-done.15), kind=kCustom, calls=%fused_computation.38 | custom fusion | bytes 1114114 | tf_op jit(solution)/shard_map/scatter | solution.py:41
  53.4 15.3 %all-to-all-start.1 = ((bf16[64,32,256]{2,1,0:T(8,128)(2,1)}), bf16[64,32,256]{2,1,0:T(8,128)(2,1)S(1)}, u32[]{:S(2)}, u32[]{:S(2)}) async-start(bf16[64,32,256]{2,1,0:T(8,128)(2,1)} %bitcast.7), calls=%async_computation.1 | async-start | bytes 2097152 | tf_op jit(solution)/shard_map/all_to_all | solution.py:47
  68.8 0.1 reduce.4
  68.9 1.2 reduce.3
  70.3 51.6 %all-to-all-done.1 = bf16[64,32,256]{2,1,0:T(8,128)(2,1)S(1)} async-done(((bf16[64,32,256]{2,1,0:T(8,128)(2,1)}), bf16[64,32,256]{2,1,0:T(8,128)(2,1)S(1)}, u32[]{:S(2)}, u32[]{:S(2)}) %all-to-all-start.1) | async-done | bytes 1048608 | tf_op jit(solution)/shard_map/all_to_all | solution.py:47
  121.9 9.5 %scatter_custom_fusion.1 = bf16[1792,256]{1,0:T(8,128)(2,1)S(1)} fusion(s32[2048]{0:T(1024)S(1)} %bitcast.81, bf16[2048,256]{1,0:T(8,128)(2,1)S(1)} %bitcast.72, bf16[]{:T(256)} %constant.8.clone.1), kind=kCustom, calls=%fused_computation.46 | custom fusion | bytes 917506 | tf_op jit(solution)/shard_map/scatter | solution.py:60
  131.4 1.7 convolution_convert_fusion.1
  133.2 0.2 all-reduce.3.cloned.1.call-start
  133.4 0.1 copy.40
  133.6 0.5 copy-done.13
  134.2 5.7 %scatter_custom_fusion.2 = bf16[2048,256]{1,0:T(8,128)(2,1)S(1)} fusion(s32[1024]{0:T(1024)S(1)} %bitcast.79, f32[128,256]{1,0:T(8,128)S(1)} %convert_element_type.72, f32[1024]{0:T(1024)S(1)} %mul.74, bf16[]{:T(256)} %constant.8.clone.1), kind=kCustom, calls=%fused_computation.36 | custom fusion | flops 524288 | bytes 1183746 | tf_op jit(solution)/shard_map/scatter | solution.py:41
  139.9 60.3 %all_to_all.29 = bf16[64,32,256]{2,1,0:T(8,128)(2,1)S(1)} all-to-all(bf16[64,32,256]{2,1,0:T(8,128)(2,1)S(1)} %bitcast.69), channel_id=1, replica_groups=mesh['dp'=8,'expert'=64] {'expert'}, dimensions={0} | all-to-all | bytes 2097152 | tf_op jit(solution)/shard_map/all_to_all | solution.py:78
  200.3 9.7 %scatter_custom_fusion.3 = bf16[1792,256]{1,0:T(8,128)(2,1)S(1)} fusion(s32[2048]{0:T(1024)S(1)} %bitcast.82, bf16[2048,256]{1,0:T(8,128)(2,1)S(1)} %bitcast.73, bf16[]{:T(256)} %constant.8.clone.1), kind=kCustom, calls=%fused_computation.44 | custom fusion | bytes 917506 | tf_op jit(solution)/shard_map/scatter | solution.py:60
  210.0 1.7 convolution_convert_fusion.2
  211.8 1.7 convolution_convert_fusion
  213.6 6.5 %reduce_sum.56 = bf16[1792,384]{1,0:T(8,128)(2,1)S(1)} reduce(bf16[8,1792,384]{2,1,0:T(8,128)(2,1)} %bitcast.68, bf16[]{:T(256)} %constant.8.clone.1), dimensions={0}, to_apply=%region_8.9 | reduce | flops 4816896 | bytes 12386306 | tf_op jit(solution)/shard_map/reduce_sum | solution.py:70
  220.1 66.8 %all-reduce.3.cloned.1.call-done = (bf16[1792,384]{1,0:T(8,128)(2,1)}, bf16[1792,384]{1,0:T(8,128)(2,1)}) async-done(((bf16[1792,384]{1,0:T(8,128)(2,1)}, bf16[1792,384]{1,0:T(8,128)(2,1)}), (bf16[1792,384]{1,0:T(8,128)(2,1)}, bf16[1792,384]{1,0:T(8,128)(2,1)})) %all-reduce.3.cloned.1.call-update) | async-done | bytes 2752528 | tf_op jit(solution)/shard_map/psum | solution.py:69
  286.9 3.4 fusion.3
  290.4 0.7 fusion.30
  291.1 0.4 copy-done.3
  291.4 0.4 copy-done.5
  291.9 0.7 fusion.9
  292.6 9.0 %gather_fusion.2 = bf16[2048,256]{1,0:T(8,128)(2,1)} fusion(bf16[1792,256]{1,0:T(8,128)(2,1)S(1)} %fusion.9, s32[2048]{0:T(1024)S(1)} %broadcast_clamp_fusion), kind=kCustom, calls=%fused_computation.2 | custom fusion | bytes 2105344 | tf_op jit(solution)/shard_map/gather | solution.py:63
  301.5 15.6 %all-to-all-start.4 = ((bf16[64,32,256]{2,1,0:T(8,128)(2,1)}), bf16[64,32,256]{2,1,0:T(8,128)(2,1)S(1)}, u32[]{:S(2)}, u32[]{:S(2)}) async-start(bf16[64,32,256]{2,1,0:T(8,128)(2,1)} %bitcast.71), calls=%async_computation.4 | async-start | bytes 2097152 | tf_op jit(solution)/shard_map/all_to_all | solution.py:91
  317.2 1.6 convolution_convert_fusion.3
  318.8 9.0 %gather_fusion = bf16[2048,256]{1,0:T(8,128)(2,1)} fusion(bf16[1792,256]{1,0:T(8,128)(2,1)S(1)} %convolution_convert_fusion.3, s32[2048]{0:T(1024)S(1)} %broadcast_clamp_fusion), kind=kCustom, calls=%fused_computation | custom fusion | bytes 2105344 | tf_op jit(solution)/shard_map/gather | solution.py:63
  327.7 41.3 %all-to-all-done.4 = bf16[64,32,256]{2,1,0:T(8,128)(2,1)S(1)} async-done(((bf16[64,32,256]{2,1,0:T(8,128)(2,1)}), bf16[64,32,256]{2,1,0:T(8,128)(2,1)S(1)}, u32[]{:S(2)}, u32[]{:S(2)}) %all-to-all-start.4) | async-done | bytes 1048608 | tf_op jit(solution)/shard_map/all_to_all | solution.py:91
  369.0 10.3 %all-to-all-start.2 = ((bf16[64,32,256]{2,1,0:T(8,128)(2,1)}), bf16[64,32,256]{2,1,0:T(8,128)(2,1)S(1)}, u32[]{:S(2)}, u32[]{:S(2)}) async-start(bf16[64,32,256]{2,1,0:T(8,128)(2,1)} %bitcast.70), calls=%async_computation.2 | async-start | bytes 2097152 | tf_op jit(solution)/shard_map/all_to_all | solution.py:77
  379.4 2.9 convolution_bitcast_fusion.1
  382.3 1.4 convolution_bitcast_fusion.2
  383.7 0.2 copy-done.9
  383.9 1.3 convolution_bitcast_fusion
  385.2 3.9 gather_fusion.3
  389.1 1.0 bitcast_reduce_fusion
  390.1 43.3 %all-to-all-done.2 = bf16[64,32,256]{2,1,0:T(8,128)(2,1)S(1)} async-done(((bf16[64,32,256]{2,1,0:T(8,128)(2,1)}), bf16[64,32,256]{2,1,0:T(8,128)(2,1)S(1)}, u32[]{:S(2)}, u32[]{:S(2)}) %all-to-all-start.2) | async-done | bytes 1048608 | tf_op jit(solution)/shard_map/all_to_all | solution.py:77
  433.4 3.9 gather_fusion.1
  437.4 1.0 fusion.10
  (53 shorter events, 0.9 us)
Async XLA Ops:
  7.2 202.8 %copy-start = (bf16[1,256,384]{2,1,0:T(8,128)(2,1)S(1)}, bf16[1,256,384]{2,1,0:T(8,128)(2,1)}, u32[]{:S(2)}) copy-start(bf16[1,256,384]{2,1,0:T(8,128)(2,1)} %param.11) | copy-start | bytes 589828
  7.2 40.1 %copy-start.15 = (bf16[128,256]{1,0:T(8,128)(2,1)S(1)}, bf16[128,256]{1,0:T(8,128)(2,1)}, u32[]{:S(2)}) copy-start(bf16[128,256]{1,0:T(8,128)(2,1)} %param.7) | copy-start | bytes 196612
  9.0 44.4 %all-to-all-start = ((s32[64,1,1]{2,1,0:T(1,128)}), s32[64,1,1]{2,1,0:T(1,128)S(1)}, u32[]{:S(2)}, u32[]{:S(2)}) async-start(s32[64,1,1]{2,1,0:T(1,128)} %copy.42), calls=%async_computation | async-start | bytes 65536 | tf_op jit(solution)/shard_map/all_to_all | solution.py:48
  53.4 78.1 %copy-start.10 = (bf16[1,256,384]{2,1,0:T(8,128)(2,1)S(1)}, bf16[1,256,384]{2,1,0:T(8,128)(2,1)}, u32[]{:S(2)}) copy-start(bf16[1,256,384]{2,1,0:T(8,128)(2,1)} %param.12) | copy-start | bytes 589828
  53.4 68.5 %all-to-all-start.1 = ((bf16[64,32,256]{2,1,0:T(8,128)(2,1)}), bf16[64,32,256]{2,1,0:T(8,128)(2,1)S(1)}, u32[]{:S(2)}, u32[]{:S(2)}) async-start(bf16[64,32,256]{2,1,0:T(8,128)(2,1)} %bitcast.7), calls=%async_computation.1 | async-start | bytes 2097152 | tf_op jit(solution)/shard_map/all_to_all | solution.py:47
  68.6 145.0 %all-gather.3.cloned.1.call-start = ((), (), s32[]{:S(2)}) async-start(), calls=%async_computation.5 | async-start | bytes 12386304 | tf_op jit(solution)/shard_map/all_gather | solution.py:70
  131.4 78.6 %copy-start.1 = (bf16[1792,256]{1,0:T(8,128)(2,1)}, bf16[1792,256]{1,0:T(8,128)(2,1)S(1)}, u32[]{:S(2)}) copy-start(bf16[1792,256]{1,0:T(8,128)(2,1)S(1)} %scatter_custom_fusion.1) | copy-start | bytes 2752516
  131.4 2.0 copy-start.17
  133.2 1.0 copy-start.16
  133.2 153.7 %all-reduce.3.cloned.1.call-start = ((), (), s32[]{:S(2)}) async-start(), calls=%async_computation.6 | async-start | bytes 5505024 | tf_op jit(solution)/shard_map/psum | solution.py:69
  133.5 0.6 copy-start.13
  210.0 3.5 copy-start.8
  210.0 1.8 copy-start.12
  290.4 1.1 copy-start.3
  290.4 1.5 copy-start.5
  290.4 26.8 %copy-start.6 = (bf16[1792,384]{1,0:T(8,128)(2,1)}, bf16[1792,384]{1,0:T(8,128)(2,1)S(1)}, u32[]{:S(2)}) copy-start(bf16[1792,384]{1,0:T(8,128)(2,1)S(1)} %get-tuple-element.9) | copy-start | bytes 4128772
  290.4 1.5 copy-start.11
  301.5 67.5 %all-to-all-start.4 = ((bf16[64,32,256]{2,1,0:T(8,128)(2,1)}), bf16[64,32,256]{2,1,0:T(8,128)(2,1)S(1)}, u32[]{:S(2)}, u32[]{:S(2)}) async-start(bf16[64,32,256]{2,1,0:T(8,128)(2,1)} %bitcast.71), calls=%async_computation.4 | async-start | bytes 2097152 | tf_op jit(solution)/shard_map/all_to_all | solution.py:91
  327.7 51.7 %copy-start.2 = (bf16[1792,256]{1,0:T(8,128)(2,1)S(1)}, bf16[1792,256]{1,0:T(8,128)(2,1)}, u32[]{:S(2)}) copy-start(bf16[1792,256]{1,0:T(8,128)(2,1)} %copy-done.1) | copy-start | bytes 2752516
  369.0 64.4 %all-to-all-start.2 = ((bf16[64,32,256]{2,1,0:T(8,128)(2,1)}), bf16[64,32,256]{2,1,0:T(8,128)(2,1)S(1)}, u32[]{:S(2)}, u32[]{:S(2)}) async-start(bf16[64,32,256]{2,1,0:T(8,128)(2,1)} %bitcast.70), calls=%async_computation.2 | async-start | bytes 2097152 | tf_op jit(solution)/shard_map/all_to_all | solution.py:77
  379.4 2.9 copy-start.4
  382.3 1.4 copy-start.7
  382.3 1.6 copy-start.9
  433.4 3.9 copy-start.14
Sparse Core Ops, SparseCore 0:
  133.3 59.0 all-gather.2
  213.7 73.1 all-reduce.2
